TPU v7x, 32 devices: a whole 2x2x4 slice. The times are simulated.
32 devices in a mesh: lat: 4 (over y, x), lon: 2 (over core), lev: 4 (over z).
Axes of the slice: x: 2, y: 2, z: 4, core: 2. Of those that a mesh axis runs over, the one named last changes fastest.
Arguments:
- winds: float32 [16, 72, 2, 256], P('lat', 'lev', None, 'lon'), may hold values from -0.45 to 0.45
- mixing: float32 [16, 72, 72], P(('lat', 'lev')), may hold values from -0.12 to 0.7, as said below
- kernels: float32 [2048, 72], P(('lat', 'lon', 'lev')), may hold values from 0.2 to 1.2
- residuals: float32 [2048, 16], P(('lat', 'lon', 'lev')), may hold values from -6 to 6
- columns: int32 [2048], P(('lat', 'lon', 'lev')), may hold values from 0 to 127
- owners: int32 [2048, 1], P(('lat', 'lon', 'lev')), may hold values from 0 to 7; in each aligned block of 64 rows (0 to 63, 64 to 127, ...) at most 16 rows name the same one
- live_counts: int32 [32], P(('lat', 'lon', 'lev')), may hold values from 32 to 64, as said below
Outputs:
- gradient: float32 [16, 72, 16, 256], P('lat', 'lev', None, 'lon')
Inputs may be any that keep to these rules, and one draw needn't show every extreme that they name: Diagonal entries of every mixing matrix lie between 0.38 and 0.7, off-diagonal entries between -0.12 and 0.12, in every draw. The first live_counts[b] slots of device b's retrievals are live; some device has all 64 live. Column index row by row over the owner's 1 row of 128 columns. `owners`: at most 16 slots of one device name the same owner.
All inputs are finite; a program needn't handle non-finite values.
Results may differ from a plain program's by a relative error of at most 0.00022.
Values sent between devices are 32-bit elements; how exact they have to be, the bound alone decides.
A program may use at most 64 MiB of HBM per device.

v0:
```python
import jax
import jax.numpy as jnp
from jax import lax
from jax.sharding import PartitionSpec as P

STEPS = 4


def with_halo(block, sides, width):
    for axis, dim in sides:
        count = lax.axis_size(axis)
        forward = [(i, i + 1) for i in range(count - 1)]
        forward.append((count - 1, 0))
        backward = [(target, source) for source, target in forward]
        low = lax.ppermute(
            lax.slice_in_dim(block, block.shape[dim] - width, None, axis=dim), axis, forward
        )
        high = lax.ppermute(lax.slice_in_dim(block, 0, width, axis=dim), axis, backward)
        block = jnp.concatenate([low, block, high], axis=dim)
    return block


def transport(padded, winds, at_first, at_last):
    centre = padded[1:-1, :, :, 1:-1]
    east_side = padded[1:-1, :, :, 2:]
    west_side = padded[1:-1, :, :, :-2]
    north_side = padded[2:, :, :, 1:-1]
    south_side = padded[:-2, :, :, 1:-1]
    north_side = jnp.concatenate([north_side[:-1], jnp.where(at_last, centre, north_side)], axis=0)
    south_side = jnp.concatenate([jnp.where(at_first, centre, south_side), south_side[1:]], axis=0)
    zonal_wind = winds[:, :, 0:1, :]
    merid_wind = winds[:, :, 1:2, :]
    return (
        centre
        + jnp.maximum(zonal_wind, 0.0) * (east_side - centre)
        + jnp.minimum(zonal_wind, 0.0) * (centre - west_side)
        + jnp.maximum(merid_wind, 0.0) * (north_side - centre)
        + jnp.minimum(merid_wind, 0.0) * (centre - south_side)
    )


def mix_back(mixing, adjoint):
    return jnp.einsum("rjk,rjtl->rktl", mixing, adjoint, precision=lax.Precision.HIGHEST)


def deposit(summed, kern_rows, resid_part, col_ids):
    contrib = (kern_rows[:, :, None] * resid_part[:, None, :]).reshape(kern_rows.shape[0], -1)
    return summed.at[col_ids].add(contrib)


def shards(winds, mixing, kernels, residuals, columns, owners, live_counts):
    levels = mixing.shape[1]
    tracers = residuals.shape[1]
    slab_rows = mixing.shape[0]
    tile_cols = winds.shape[3]
    row_count = kernels.shape[0]
    lat_size = lax.axis_size("lat")
    lev_size = lax.axis_size("lev")
    my_index = lax.axis_index("lon") * lev_size + lax.axis_index("lev")
    live_mask = (jnp.arange(row_count) < live_counts[0]).astype(jnp.float32)
    resid_rows = residuals * live_mask[:, None]
    owner_ids = owners[:, 0]
    running = jnp.zeros((slab_rows * tile_cols, levels * tracers), jnp.float32)
    kern_part = lax.all_gather(kernels, ("lon", "lev"), axis=0, tiled=True)
    resid_part = lax.all_gather(resid_rows, ("lon", "lev"), axis=0, tiled=True)
    col_part = lax.all_gather(columns, ("lon", "lev"), axis=0, tiled=True)
    owner_part = lax.all_gather(owner_ids, ("lon", "lev"), axis=0, tiled=True)
    keep_mask = (owner_part == my_index).astype(jnp.float32)
    running = deposit(running, kern_part, resid_part * keep_mask[:, None], col_part)
    adjoint = running.reshape(slab_rows, tile_cols, levels, tracers).transpose(0, 2, 3, 1)
    wind_cols = lax.all_to_all(winds, "lev", split_axis=0, concat_axis=1, tiled=True)
    lat_pos = lax.axis_index("lat")
    lev_pos = lax.axis_index("lev")
    at_first = (lat_pos == 0) & (lev_pos == 0)
    at_last = (lat_pos == lat_size - 1) & (lev_pos == lev_size - 1)
    for sweep_index in range(STEPS):
        mixed = mix_back(mixing, adjoint)
        padded = with_halo(mixed, ((("lat", "lev"), 0), ("lon", 3)), 1)
        adjoint = transport(padded, wind_cols, at_first, at_last)
    gradient = lax.all_to_all(adjoint, "lev", split_axis=1, concat_axis=0, tiled=True)
    return gradient


def solution(mesh):
    return jax.shard_map(
        shards,
        mesh=mesh,
        in_specs=(
            P("lat", "lev", None, "lon"),
            P(("lat", "lev"), None, None),
            P(("lat", "lon", "lev"), None),
            P(("lat", "lon", "lev"), None),
            P(("lat", "lon", "lev")),
            P(("lat", "lon", "lev"), None),
            P(("lat", "lon", "lev")),
        ),
        out_specs=P("lat", "lev", None, "lon"),
        check_vma=False,
    )
```

profile of v0, /device:TPU:0, one launch (start us, length us, event | category | flops | bytes accessed | tf_op | source)
XLA Modules:
  0.0 261.8 jit_solution(14220002208314231462)
XLA Ops:
  0.7 1.2 dynamic-slice
  2.6 0.9 dynamic-update-slice
  3.4 0.7 bitcast_dynamic-update-slice_fusion
  4.2 10.7 %all-reduce.2 = (s32[512]{0:T(512)S(1)}, s32[512]{0:T(512)S(1)}) all-reduce(s32[512]{0:T(512)S(1)} %dynamic-update-slice, s32[512]{0:T(512)S(1)} %bitcast_dynamic-update-slice_fusion), channel_id=1, replica_groups=mesh['lat'=4,'lon'=2,'lev'=4] {'lon','lev'}, use_global_device_ids=true, to_apply=%add | all-reduce | flops 1024 | bytes 8192
  14.9 0.7 multiply_bitcast_fusion
  15.6 23.9 %all-gather.1 = f32[8,64,16]{1,2,0:T(8,128)S(1)} all-gather(f32[1,64,16]{1,2,0:T(8,128)S(1)} %multiply_bitcast_fusion), channel_id=1, replica_groups=mesh['lat'=4,'lon'=2,'lev'=4] {'lon','lev'}, dimensions={0}, use_global_device_ids=true | all-gather | bytes 36864 | tf_op jit(solution)/shard_map/all_gather | solution.py:65
  39.6 25.4 %all_gather.13 = f32[512,72]{1,0:T(8,128)S(1)} all-gather(f32[64,72]{1,0:T(8,128)} %param.9), channel_id=1, replica_groups=mesh['lat'=4,'lon'=2,'lev'=4] {'lon','lev'}, dimensions={0}, use_global_device_ids=true | all-gather | bytes 165888 | tf_op jit(solution)/shard_map/all_gather | solution.py:64
  65.2 0.3 broadcast_multiply_fusion
  65.5 2.0 copy.39
  67.5 6.4 %scatter_custom_fusion = f32[128,1152]{1,0:T(8,128)S(1)} fusion(s32[512]{0:T(512)S(1)} %compare_select_fusion, f32[512,1152]{1,0:T(8,128)} %copy.39, f32[]{:T(128)} %constant.8.clone.1), kind=kCustom, calls=%fused_computation.104 | custom fusion | flops 589824 | bytes 590336 | tf_op jit(solution)/shard_map/scatter-add | solution.py:48
  74.0 0.2 copy.40
  74.2 0.8 convolution_bitcast_fusion.3
  75.1 3.5 %collective-permute-start.1 = (f32[1,72,16,128]{3,1,2,0:T(8,128)S(1)}, f32[1,72,16,128]{3,1,2,0:T(8,128)S(1)}, u32[]{:S(2)}, u32[]{:S(2)}) collective-permute-start(f32[1,72,16,128]{3,1,2,0:T(8,128)S(1)} %convolution_bitcast_fusion.3), channel_id=1, source_target_pairs={{1,0},{2,1},{3,2},{8,3},{9,8},{10,9},{11,10},{16,11},{17,16},{18,1... | collective-permute-start | bytes 1769480 | tf_op jit(solution)/shard_map/ppermute | solution.py:18
  78.6 4.1 %all-to-all-start = ((f32[4,18,2,128]{3,2,1,0:T(2,128)}), f32[4,18,2,128]{3,2,1,0:T(2,128)S(1)}, u32[]{:S(2)}, u32[]{:S(2)}) async-start(f32[4,18,2,128]{3,2,1,0:T(2,128)} %param.7), calls=%async_computation | async-start | bytes 147456 | tf_op jit(solution)/shard_map/all_to_all | solution.py:71
  82.7 22.6 %all-to-all-done = f32[4,18,2,128]{3,2,1,0:T(2,128)S(1)} async-done(((f32[4,18,2,128]{3,2,1,0:T(2,128)}), f32[4,18,2,128]{3,2,1,0:T(2,128)S(1)}, u32[]{:S(2)}, u32[]{:S(2)}) %all-to-all-start) | async-done | bytes 73760 | tf_op jit(solution)/shard_map/all_to_all | solution.py:71
  105.5 0.3 collective-permute-done
  105.7 0.5 copy-done.1
  106.3 0.8 copy-done.2
  107.2 1.8 fusion.92
  109.0 2.0 copy.44
  111.0 0.6 copy.46
  111.7 0.5 collective-permute-start.2
  112.2 0.8 collective-permute-done.2
  113.0 0.6 copy.45
  113.6 1.9 copy.47
  115.5 2.7 %convolution_bitcast_fusion.2 = f32[1,72,16,128]{3,1,2,0:T(8,128)S(1)} fusion(f32[1,72,16,128]{3,1,2,0:T(8,128)S(1)} %convolution_bitcast_fusion.3, f32[1,72,16,128]{3,1,2,0:T(8,128)} %copy-done.1, f32[1,72,16,128]{3,1,2,0:T(8,128)} %copy-done.2, f32[3,72,16,1]{3,1,2,0:T(8,128)} %copy.47, f32[3,72,16,1]{3,1,2,0:T(8,128)S(1)} %copy.45, ...), kind=kOutput, calls=%fused_computation.7 | convolution fusion | flops 130351104 | bytes 2555138 | tf_op jit(solution)/shard_map/rjk,rjtl->rktl/dot_general | solution.py:43
  118.2 4.1 %collective-permute-start.5 = (f32[1,72,16,128]{3,1,2,0:T(8,128)S(1)}, f32[1,72,16,128]{3,1,2,0:T(8,128)S(1)}, u32[]{:S(2)}, u32[]{:S(2)}) collective-permute-start(f32[1,72,16,128]{3,1,2,0:T(8,128)S(1)} %convolution_bitcast_fusion.2), channel_id=1, source_target_pairs={{1,0},{2,1},{3,2},{8,3},{9,8},{10,9},{11,10},{16,11},{17,16},{18,1... | collective-permute-start | bytes 1769480 | tf_op jit(solution)/shard_map/ppermute | solution.py:18
  122.3 13.7 %collective-permute-done.5 = f32[1,72,16,128]{3,1,2,0:T(8,128)S(1)} collective-permute-done((f32[1,72,16,128]{3,1,2,0:T(8,128)S(1)}, f32[1,72,16,128]{3,1,2,0:T(8,128)S(1)}, u32[]{:S(2)}, u32[]{:S(2)}) %collective-permute-start.5) | collective-permute-done | bytes 589856 | tf_op jit(solution)/shard_map/ppermute | solution.py:18
  136.0 13.2 %collective-permute-done.4 = f32[1,72,16,128]{3,1,2,0:T(8,128)S(1)} collective-permute-done((f32[1,72,16,128]{3,1,2,0:T(8,128)S(1)}, f32[1,72,16,128]{3,1,2,0:T(8,128)S(1)}, u32[]{:S(2)}, u32[]{:S(2)}) %collective-permute-start.4) | collective-permute-done | bytes 589856 | tf_op jit(solution)/shard_map/ppermute | solution.py:15
  149.2 0.8 copy-done.6
  150.2 1.8 fusion.91
  152.0 2.0 copy.50
  154.1 0.6 copy.52
  154.7 0.5 collective-permute-start.7
  155.3 0.6 copy.51
  156.1 1.9 copy.53
  157.9 2.7 %convolution_bitcast_fusion.1 = f32[1,72,16,128]{3,1,2,0:T(8,128)S(1)} fusion(f32[1,72,16,128]{3,1,2,0:T(8,128)S(1)} %convolution_bitcast_fusion.2, f32[1,72,16,128]{3,1,2,0:T(8,128)} %copy-done.4, f32[1,72,16,128]{3,1,2,0:T(8,128)} %copy-done.6, f32[3,72,16,1]{3,1,2,0:T(8,128)} %copy.53, f32[3,72,16,1]{3,1,2,0:T(8,128)S(1)} %copy.51, ...), kind=kOutput, calls=%fused_computation.6 | convolution fusion | flops 130351104 | bytes 2555138 | tf_op jit(solution)/shard_map/rjk,rjtl->rktl/dot_general | solution.py:43
  160.6 1.8 collective-permute-start.9
  162.4 0.3 collective-permute-start.8
  162.7 13.8 %collective-permute-done.9 = f32[1,72,16,128]{3,1,2,0:T(8,128)S(1)} collective-permute-done((f32[1,72,16,128]{3,1,2,0:T(8,128)S(1)}, f32[1,72,16,128]{3,1,2,0:T(8,128)S(1)}, u32[]{:S(2)}, u32[]{:S(2)}) %collective-permute-start.9) | collective-permute-done | bytes 589856 | tf_op jit(solution)/shard_map/ppermute | solution.py:18
  176.5 12.8 %collective-permute-done.8 = f32[1,72,16,128]{3,1,2,0:T(8,128)S(1)} collective-permute-done((f32[1,72,16,128]{3,1,2,0:T(8,128)S(1)}, f32[1,72,16,128]{3,1,2,0:T(8,128)S(1)}, u32[]{:S(2)}, u32[]{:S(2)}) %collective-permute-start.8) | collective-permute-done | bytes 589856 | tf_op jit(solution)/shard_map/ppermute | solution.py:15
  189.3 0.8 copy-done.7
  190.2 1.8 fusion.90
  192.1 2.0 copy.55
  194.1 0.6 copy.57
  194.7 0.5 collective-permute-start.11
  195.3 0.6 copy.56
  196.1 1.9 copy.58
  197.9 2.7 %convolution_bitcast_fusion = f32[1,72,16,128]{3,1,2,0:T(8,128)S(1)} fusion(f32[1,72,16,128]{3,1,2,0:T(8,128)S(1)} %convolution_bitcast_fusion.1, f32[1,72,16,128]{3,1,2,0:T(8,128)} %copy-done.5, f32[1,72,16,128]{3,1,2,0:T(8,128)} %copy-done.7, f32[3,72,16,1]{3,1,2,0:T(8,128)} %copy.58, f32[3,72,16,1]{3,1,2,0:T(8,128)S(1)} %copy.56, ...), kind=kOutput, calls=%fused_computation.5 | convolution fusion | flops 130351104 | bytes 2555138 | tf_op jit(solution)/shard_map/rjk,rjtl->rktl/dot_general | solution.py:43
  200.6 2.7 %collective-permute-start.13 = (f32[1,72,16,128]{3,1,2,0:T(8,128)S(1)}, f32[1,72,16,128]{3,1,2,0:T(8,128)S(1)}, u32[]{:S(2)}, u32[]{:S(2)}) collective-permute-start(f32[1,72,16,128]{3,1,2,0:T(8,128)S(1)} %convolution_bitcast_fusion), channel_id=1, source_target_pairs={{1,0},{2,1},{3,2},{8,3},{9,8},{10,9},{11,10},{16,11},{17,16},{18,1... | collective-permute-start | bytes 1769480 | tf_op jit(solution)/shard_map/ppermute | solution.py:18
  203.4 13.7 %collective-permute-done.13 = f32[1,72,16,128]{3,1,2,0:T(8,128)S(1)} collective-permute-done((f32[1,72,16,128]{3,1,2,0:T(8,128)S(1)}, f32[1,72,16,128]{3,1,2,0:T(8,128)S(1)}, u32[]{:S(2)}, u32[]{:S(2)}) %collective-permute-start.13) | collective-permute-done | bytes 589856 | tf_op jit(solution)/shard_map/ppermute | solution.py:18
  217.1 14.2 %collective-permute-done.12 = f32[1,72,16,128]{3,1,2,0:T(8,128)S(1)} collective-permute-done((f32[1,72,16,128]{3,1,2,0:T(8,128)S(1)}, f32[1,72,16,128]{3,1,2,0:T(8,128)S(1)}, u32[]{:S(2)}, u32[]{:S(2)}) %collective-permute-start.12) | collective-permute-done | bytes 589856 | tf_op jit(solution)/shard_map/ppermute | solution.py:15
  231.3 0.8 copy-done.3
  232.1 0.2 pad_maximum_fusion.3
  232.3 1.8 fusion.89
  234.1 2.0 copy.60
  236.2 0.6 copy.62
  236.8 0.5 collective-permute-start.15
  237.4 0.6 copy.61
  238.0 0.2 collective-permute-done.15
  238.1 1.9 copy.63
  240.0 1.8 fusion.23
  241.9 19.1 %all_to_all.24 = f32[1,72,16,128]{3,2,0,1:T(8,128)S(1)} all-to-all(f32[1,72,16,128]{3,2,0,1:T(8,128)S(1)} %copy.64), channel_id=1, replica_groups=mesh['lat'=4,'lon'=2,'lev'=4] {'lev'}, dimensions={1} | all-to-all | bytes 1179648 | tf_op jit(solution)/shard_map/all_to_all | solution.py:80
  261.0 0.8 copy.83
  (40 shorter events, 1.7 us)
Async XLA Ops:
  0.0 74.2 %copy-start = (f32[1,72,72]{2,1,0:T(8,128)S(1)}, f32[1,72,72]{2,1,0:T(8,128)}, u32[]{:S(2)}) copy-start(f32[1,72,72]{2,1,0:T(8,128)} %param.8) | copy-start | bytes 62212
  75.1 30.3 %collective-permute-start.1 = (f32[1,72,16,128]{3,1,2,0:T(8,128)S(1)}, f32[1,72,16,128]{3,1,2,0:T(8,128)S(1)}, u32[]{:S(2)}, u32[]{:S(2)}) collective-permute-start(f32[1,72,16,128]{3,1,2,0:T(8,128)S(1)} %convolution_bitcast_fusion.3), channel_id=1, source_target_pairs={{1,0},{2,1},{3,2},{8,3},{9,8},{10,9},{11,10},{16,11},{17,16},{18,1... | collective-permute-start | bytes 1769480 | tf_op jit(solution)/shard_map/ppermute | solution.py:18
  78.6 27.1 %collective-permute-start = (f32[1,72,16,128]{3,1,2,0:T(8,128)S(1)}, f32[1,72,16,128]{3,1,2,0:T(8,128)S(1)}, u32[]{:S(2)}, u32[]{:S(2)}) collective-permute-start(f32[1,72,16,128]{3,1,2,0:T(8,128)S(1)} %convolution_bitcast_fusion.3), channel_id=1, source_target_pairs={{0,1},{1,2},{2,3},{3,8},{8,9},{9,10},{10,11},{11,16},{16,17},{17,1... | collective-permute-start | bytes 1769480 | tf_op jit(solution)/shard_map/ppermute | solution.py:15
  78.6 26.7 %all-to-all-start = ((f32[4,18,2,128]{3,2,1,0:T(2,128)}), f32[4,18,2,128]{3,2,1,0:T(2,128)S(1)}, u32[]{:S(2)}, u32[]{:S(2)}) async-start(f32[4,18,2,128]{3,2,1,0:T(2,128)} %param.7), calls=%async_computation | async-start | bytes 147456 | tf_op jit(solution)/shard_map/all_to_all | solution.py:71
  105.4 0.8 copy-start.1
  106.3 0.8 copy-start.2
  111.6 2.0 collective-permute-start.3
  111.7 1.3 collective-permute-start.2
  118.2 17.8 %collective-permute-start.5 = (f32[1,72,16,128]{3,1,2,0:T(8,128)S(1)}, f32[1,72,16,128]{3,1,2,0:T(8,128)S(1)}, u32[]{:S(2)}, u32[]{:S(2)}) collective-permute-start(f32[1,72,16,128]{3,1,2,0:T(8,128)S(1)} %convolution_bitcast_fusion.2), channel_id=1, source_target_pairs={{1,0},{2,1},{3,2},{8,3},{9,8},{10,9},{11,10},{16,11},{17,16},{18,1... | collective-permute-start | bytes 1769480 | tf_op jit(solution)/shard_map/ppermute | solution.py:18
  122.3 27.0 %collective-permute-start.4 = (f32[1,72,16,128]{3,1,2,0:T(8,128)S(1)}, f32[1,72,16,128]{3,1,2,0:T(8,128)S(1)}, u32[]{:S(2)}, u32[]{:S(2)}) collective-permute-start(f32[1,72,16,128]{3,1,2,0:T(8,128)S(1)} %convolution_bitcast_fusion.2), channel_id=1, source_target_pairs={{0,1},{1,2},{2,3},{3,8},{8,9},{9,10},{10,11},{11,16},{16,17},{17,1... | collective-permute-start | bytes 1769480 | tf_op jit(solution)/shard_map/ppermute | solution.py:15
  136.0 13.2 %copy-start.4 = (f32[1,72,16,128]{3,1,2,0:T(8,128)}, f32[1,72,16,128]{3,1,2,0:T(8,128)S(1)}, u32[]{:S(2)}) copy-start(f32[1,72,16,128]{3,1,2,0:T(8,128)S(1)} %collective-permute-done.5) | copy-start | bytes 1769476
  149.2 0.8 copy-start.6
  154.1 1.2 collective-permute-start.6
  154.7 1.4 collective-permute-start.7
  160.6 15.9 %collective-permute-start.9 = (f32[1,72,16,128]{3,1,2,0:T(8,128)S(1)}, f32[1,72,16,128]{3,1,2,0:T(8,128)S(1)}, u32[]{:S(2)}, u32[]{:S(2)}) collective-permute-start(f32[1,72,16,128]{3,1,2,0:T(8,128)S(1)} %convolution_bitcast_fusion.1), channel_id=1, source_target_pairs={{1,0},{2,1},{3,2},{8,3},{9,8},{10,9},{11,10},{16,11},{17,16},{18,1... | collective-permute-start | bytes 1769480 | tf_op jit(solution)/shard_map/ppermute | solution.py:18
  162.4 26.9 %collective-permute-start.8 = (f32[1,72,16,128]{3,1,2,0:T(8,128)S(1)}, f32[1,72,16,128]{3,1,2,0:T(8,128)S(1)}, u32[]{:S(2)}, u32[]{:S(2)}) collective-permute-start(f32[1,72,16,128]{3,1,2,0:T(8,128)S(1)} %convolution_bitcast_fusion.1), channel_id=1, source_target_pairs={{0,1},{1,2},{2,3},{3,8},{8,9},{9,10},{10,11},{11,16},{16,17},{17,1... | collective-permute-start | bytes 1769480 | tf_op jit(solution)/shard_map/ppermute | solution.py:15
  176.5 12.8 %copy-start.5 = (f32[1,72,16,128]{3,1,2,0:T(8,128)}, f32[1,72,16,128]{3,1,2,0:T(8,128)S(1)}, u32[]{:S(2)}) copy-start(f32[1,72,16,128]{3,1,2,0:T(8,128)S(1)} %collective-permute-done.9) | copy-start | bytes 1769476
  189.3 0.8 copy-start.7
  194.1 1.2 collective-permute-start.10
  194.7 1.4 collective-permute-start.11
  200.6 16.4 %collective-permute-start.13 = (f32[1,72,16,128]{3,1,2,0:T(8,128)S(1)}, f32[1,72,16,128]{3,1,2,0:T(8,128)S(1)}, u32[]{:S(2)}, u32[]{:S(2)}) collective-permute-start(f32[1,72,16,128]{3,1,2,0:T(8,128)S(1)} %convolution_bitcast_fusion), channel_id=1, source_target_pairs={{1,0},{2,1},{3,2},{8,3},{9,8},{10,9},{11,10},{16,11},{17,16},{18,1... | collective-permute-start | bytes 1769480 | tf_op jit(solution)/shard_map/ppermute | solution.py:18
  203.3 27.9 %collective-permute-start.12 = (f32[1,72,16,128]{3,1,2,0:T(8,128)S(1)}, f32[1,72,16,128]{3,1,2,0:T(8,128)S(1)}, u32[]{:S(2)}, u32[]{:S(2)}) collective-permute-start(f32[1,72,16,128]{3,1,2,0:T(8,128)S(1)} %convolution_bitcast_fusion), channel_id=1, source_target_pairs={{0,1},{1,2},{2,3},{3,8},{8,9},{9,10},{10,11},{11,16},{16,17},{17,1... | collective-permute-start | bytes 1769480 | tf_op jit(solution)/shard_map/ppermute | solution.py:15
  231.3 0.8 copy-start.3
  236.1 1.2 collective-permute-start.14
  236.8 1.4 collective-permute-start.15
where the time goes:
time: 262 us
  waiting for transfers between devices  106 us (40%)
  blocking collectives  79.2 us (30%)
  local copies, waits for them, and re-layouts  37.5 us (14%)
  starting transfers between devices  18.9 us (7%)
  other arithmetic  9.9 us (4%)
  matrix products  8.81 us (3%)
    ppermute x8, waiting for transfers between devices, with_halo(): lax.ppermute(lax.slice_in_dim(block, 0, width, axis=dim), axis, backward)  42.3 us
    ppermute x8, waiting for transfers between devices, with_halo(): lax.ppermute(lax.slice_in_dim(block, block.shape[dim] - width, None, axis...  41 us
    all_gather x1, blocking collectives, shards(): kern_part = lax.all_gather(kernels, ('lon', 'lev'), axis=0, tiled=True)  25.4 us
    all_gather x1, blocking collectives, shards(): resid_part = lax.all_gather(resid_rows, ('lon', 'lev'), axis=0, tiled=True)  23.9 us
    all_to_all x1, waiting for transfers between devices, shards(): lax.all_to_all(winds, 'lev', split_axis=0, concat_axis=1, tiled=True)  22.6 us
    all_to_all x1, blocking collectives, shards(): lax.all_to_all(adjoint, 'lev', split_axis=1, concat_axis=0, tiled=True)  19.1 us
    slice x8, local copies, waits for them, and re-layouts, with_halo(): lax.slice_in_dim(block, 0, width, axis=dim)  15.4 us
    ppermute x8, starting transfers between devices, with_halo(): lax.ppermute(lax.slice_in_dim(block, 0, width, axis=dim), axis, backward)  12.8 us
  transfers between devices with their start and end apart: 17, of which 15 were waited for; matrix products, arithmetic and copies ran while one was open for 2% of the time, Pallas kernels for 0%

commit v1 on v0

--- a/solution.py
+++ b/solution.py
@@ -62,7 +62,28 @@
     owner_ids = owners[:, 0]
     running = jnp.zeros((slab_rows * tile_cols, levels * tracers), jnp.float32)
     kern_part = lax.all_gather(kernels, ("lon", "lev"), axis=0, tiled=True)
-    resid_part = lax.all_gather(resid_rows, ("lon", "lev"), axis=0, tiled=True)
+    size, place, rows = (
+        lax.axis_size(("lon", "lev")),
+        lax.axis_index(("lon", "lev")),
+        resid_rows.shape[0],
+    )
+    ahead = [(i_2, (i_2 + 1) % size) for i_2 in range(size)]
+    left = [(i_2, (i_2 - 1) % size) for i_2 in range(size)]
+    out = jnp.zeros(
+        (*resid_rows.shape[:0], size * rows, *resid_rows.shape[0 + 1 :]), resid_rows.dtype
+    )
+    out = lax.dynamic_update_slice_in_dim(out, resid_rows, place * rows, axis=0)
+    from_left = from_right = resid_rows
+    middle = size // 2
+    for step in range(1, middle + 1):
+        from_left = lax.ppermute(from_left, ("lon", "lev"), ahead)
+        out = lax.dynamic_update_slice_in_dim(out, from_left, (place - step) % size * rows, axis=0)
+        if step < size - middle:
+            from_right = lax.ppermute(from_right, ("lon", "lev"), left)
+            out = lax.dynamic_update_slice_in_dim(
+                out, from_right, (place + step) % size * rows, axis=0
+            )
+    resid_part = out
     col_part = lax.all_gather(columns, ("lon", "lev"), axis=0, tiled=True)
     owner_part = lax.all_gather(owner_ids, ("lon", "lev"), axis=0, tiled=True)
     keep_mask = (owner_part == my_index).astype(jnp.float32)

time: 262 us -> 255 us (0.973)
  blocking collectives: 79.2 us -> 53.9 us
  starting transfers between devices: 18.9 us -> 30.1 us
  waiting for transfers between devices: 106 us -> 110 us
    all_gather x1 -> x0, blocking collectives: 23.9 us -> none  [shards(): resid_part = lax.all_gather(resid_rows, ('lon', 'lev'), axis=0, tiled=True)]
    ppermute x0 -> x7, starting transfers between devices: none -> 11.3 us  [the longest x3 8.68 us: shards(): from_right = lax.ppermute(from_right, ('lon', 'lev'), left)]
    ppermute x0 -> x7, waiting for transfers between devices: none -> 4.25 us  [the longest x4 2.62 us: shards(): from_left = lax.ppermute(from_left, ('lon', 'lev'), ahead)]
    unnamed x23 -> x22, local copies, waits for them, and re-layouts: 7.56 us -> 7.78 us
  transfers between devices with their start and end apart: 17 -> 24, of which waited for: 15 -> 16; matrix products, arithmetic and copies ran while one was open for 2% -> 4% of each run, Pallas kernels for 0% -> 0%
where the time goes in v1:
time: 255 us; the launch traced here: 254 us
  waiting for transfers between devices  110 us (43%)
  blocking collectives  53.9 us (21%)
  local copies, waits for them, and re-layouts  39.8 us (16%)
  starting transfers between devices  30.1 us (12%)
  other arithmetic  9.9 us (4%)
  matrix products  8.81 us (3%)
    ppermute x8, waiting for transfers between devices, with_halo(): lax.ppermute(lax.slice_in_dim(block, 0, width, axis=dim), axis, backward)  42.5 us
    ppermute x8, waiting for transfers between devices, with_halo(): lax.ppermute(lax.slice_in_dim(block, block.shape[dim] - width, None, axis...  40.4 us
    all_gather x1, blocking collectives, shards(): kern_part = lax.all_gather(kernels, ('lon', 'lev'), axis=0, tiled=True)  25.5 us
    all_to_all x1, waiting for transfers between devices, shards(): lax.all_to_all(winds, 'lev', split_axis=0, concat_axis=1, tiled=True)  22.7 us
    all_to_all x1, blocking collectives, shards(): lax.all_to_all(adjoint, 'lev', split_axis=1, concat_axis=0, tiled=True)  19.1 us
    slice x8, local copies, waits for them, and re-layouts, with_halo(): lax.slice_in_dim(block, 0, width, axis=dim)  15.3 us
    ppermute x8, starting transfers between devices, with_halo(): lax.ppermute(lax.slice_in_dim(block, 0, width, axis=dim), axis, backward)  12.7 us
    unnamed x1, blocking collectives  9.34 us
  transfers between devices with their start and end apart: 24, of which 16 were waited for; matrix products, arithmetic and copies ran while one was open for 4% of the time, Pallas kernels for 0%

profile of v1, /device:TPU:0, one launch (start us, length us, event | category | flops | bytes accessed | tf_op | source)
XLA Modules:
  0.0 254.0 jit_solution(2032868492971986656)
XLA Ops:
  0.7 0.7 broadcast_multiply_fusion.2
  1.4 4.5 %collective-permute-start.1 = (f32[64,16]{0,1:T(8,128)S(1)}, f32[64,16]{0,1:T(8,128)S(1)}, u32[]{:S(2)}, u32[]{:S(2)}) collective-permute-start(f32[64,16]{0,1:T(8,128)S(1)} %broadcast_multiply_fusion.2), channel_id=1, source_target_pairs={{0,7},{1,0},{2,1},{3,2},{4,3},{5,4},{6,5},{7,6},{8,15},{9,8},{10,9... | collective-permute-start | bytes 12296 | tf_op jit(solution)/shard_map/ppermute | solution.py:82
  5.9 1.2 dynamic-slice
  7.8 0.9 dynamic-update-slice
  8.6 0.7 bitcast_dynamic-update-slice_fusion
  9.4 9.3 %all-reduce.2 = (s32[512]{0:T(512)S(1)}, s32[512]{0:T(512)S(1)}) all-reduce(s32[512]{0:T(512)S(1)} %dynamic-update-slice, s32[512]{0:T(512)S(1)} %bitcast_dynamic-update-slice_fusion), channel_id=1, replica_groups=mesh['lat'=4,'lon'=2,'lev'=4] {'lon','lev'}, use_global_device_ids=true, to_apply=%add | all-reduce | flops 1024 | bytes 8192
  18.7 2.1 collective-permute-start.2
  20.8 25.5 %all_gather.10 = f32[512,72]{1,0:T(8,128)S(1)} all-gather(f32[64,72]{1,0:T(8,128)} %param.9), channel_id=1, replica_groups=mesh['lat'=4,'lon'=2,'lev'=4] {'lon','lev'}, dimensions={0}, use_global_device_ids=true | all-gather | bytes 165888 | tf_op jit(solution)/shard_map/all_gather | solution.py:64
  46.3 1.5 collective-permute-start.3
  47.8 0.5 collective-permute-start.4
  48.3 1.6 collective-permute-done.3
  49.9 2.7 %collective-permute-start.5 = (f32[64,16]{0,1:T(8,128)S(1)}, f32[64,16]{0,1:T(8,128)S(1)}, u32[]{:S(2)}, u32[]{:S(2)}) collective-permute-start(f32[64,16]{0,1:T(8,128)S(1)} %collective-permute-done.3), channel_id=1, source_target_pairs={{0,7},{1,0},{2,1},{3,2},{4,3},{5,4},{6,5},{7,6},{8,15},{9,8},{10,9... | collective-permute-start | bytes 12296 | tf_op jit(solution)/shard_map/ppermute | solution.py:82
  54.9 2.6 %collective-permute-done.6 = f32[64,16]{0,1:T(8,128)S(1)} collective-permute-done((f32[64,16]{0,1:T(8,128)S(1)}, f32[64,16]{0,1:T(8,128)S(1)}, u32[]{:S(2)}, u32[]{:S(2)}) %collective-permute-start.6) | collective-permute-done | bytes 4128 | tf_op jit(solution)/shard_map/ppermute | solution.py:79
  58.0 2.0 copy.44
  60.0 6.4 %scatter_custom_fusion = f32[128,1152]{1,0:T(8,128)S(1)} fusion(s32[512]{0:T(512)S(1)} %compare_select_fusion, f32[512,1152]{1,0:T(8,128)} %copy.44, f32[]{:T(128)} %constant.59.clone.1), kind=kCustom, calls=%fused_computation.104 | custom fusion | flops 589824 | bytes 590336 | tf_op jit(solution)/shard_map/scatter-add | solution.py:48
  66.7 0.8 convolution_bitcast_fusion.3
  67.5 3.3 %collective-permute-start.8 = (f32[1,72,16,128]{3,1,2,0:T(8,128)S(1)}, f32[1,72,16,128]{3,1,2,0:T(8,128)S(1)}, u32[]{:S(2)}, u32[]{:S(2)}) collective-permute-start(f32[1,72,16,128]{3,1,2,0:T(8,128)S(1)} %convolution_bitcast_fusion.3), channel_id=1, source_target_pairs={{1,0},{2,1},{3,2},{8,3},{9,8},{10,9},{11,10},{16,11},{17,16},{18,1... | collective-permute-start | bytes 1769480 | tf_op jit(solution)/shard_map/ppermute | solution.py:18
  70.8 4.1 %all-to-all-start = ((f32[4,18,2,128]{3,2,1,0:T(2,128)}), f32[4,18,2,128]{3,2,1,0:T(2,128)S(1)}, u32[]{:S(2)}, u32[]{:S(2)}) async-start(f32[4,18,2,128]{3,2,1,0:T(2,128)} %param.7), calls=%async_computation | async-start | bytes 147456 | tf_op jit(solution)/shard_map/all_to_all | solution.py:92
  74.9 22.7 %all-to-all-done = f32[4,18,2,128]{3,2,1,0:T(2,128)S(1)} async-done(((f32[4,18,2,128]{3,2,1,0:T(2,128)}), f32[4,18,2,128]{3,2,1,0:T(2,128)S(1)}, u32[]{:S(2)}, u32[]{:S(2)}) %all-to-all-start) | async-done | bytes 73760 | tf_op jit(solution)/shard_map/all_to_all | solution.py:92
  97.7 0.8 copy-done.1
  98.4 0.8 copy-done.2
  99.4 1.8 fusion.92
  101.2 2.0 copy.49
  103.2 0.6 copy.51
  103.9 0.5 collective-permute-start.9
  104.4 0.8 collective-permute-done.9
  105.2 0.6 copy.50
  105.8 1.8 copy.52
  107.7 2.7 %convolution_bitcast_fusion.2 = f32[1,72,16,128]{3,1,2,0:T(8,128)S(1)} fusion(f32[1,72,16,128]{3,1,2,0:T(8,128)S(1)} %convolution_bitcast_fusion.3, f32[1,72,16,128]{3,1,2,0:T(8,128)} %copy-done.1, f32[1,72,16,128]{3,1,2,0:T(8,128)} %copy-done.2, f32[3,72,16,1]{3,1,2,0:T(8,128)} %copy.52, f32[3,72,16,1]{3,1,2,0:T(8,128)S(1)} %copy.50, ...), kind=kOutput, calls=%fused_computation.7 | convolution fusion | flops 130351104 | bytes 2555138 | tf_op jit(solution)/shard_map/rjk,rjtl->rktl/dot_general | solution.py:43
  110.3 4.1 %collective-permute-start.12 = (f32[1,72,16,128]{3,1,2,0:T(8,128)S(1)}, f32[1,72,16,128]{3,1,2,0:T(8,128)S(1)}, u32[]{:S(2)}, u32[]{:S(2)}) collective-permute-start(f32[1,72,16,128]{3,1,2,0:T(8,128)S(1)} %convolution_bitcast_fusion.2), channel_id=1, source_target_pairs={{1,0},{2,1},{3,2},{8,3},{9,8},{10,9},{11,10},{16,11},{17,16},{18,1... | collective-permute-start | bytes 1769480 | tf_op jit(solution)/shard_map/ppermute | solution.py:18
  114.5 13.7 %collective-permute-done.12 = f32[1,72,16,128]{3,1,2,0:T(8,128)S(1)} collective-permute-done((f32[1,72,16,128]{3,1,2,0:T(8,128)S(1)}, f32[1,72,16,128]{3,1,2,0:T(8,128)S(1)}, u32[]{:S(2)}, u32[]{:S(2)}) %collective-permute-start.12) | collective-permute-done | bytes 589856 | tf_op jit(solution)/shard_map/ppermute | solution.py:18
  128.2 13.2 %collective-permute-done.11 = f32[1,72,16,128]{3,1,2,0:T(8,128)S(1)} collective-permute-done((f32[1,72,16,128]{3,1,2,0:T(8,128)S(1)}, f32[1,72,16,128]{3,1,2,0:T(8,128)S(1)}, u32[]{:S(2)}, u32[]{:S(2)}) %collective-permute-start.11) | collective-permute-done | bytes 589856 | tf_op jit(solution)/shard_map/ppermute | solution.py:15
  141.4 0.8 copy-done.6
  142.4 1.8 fusion.91
  144.2 2.0 copy.55
  146.3 0.6 copy.57
  146.9 0.5 collective-permute-start.14
  147.5 0.6 copy.56
  148.2 1.8 copy.58
  150.1 2.7 %convolution_bitcast_fusion.1 = f32[1,72,16,128]{3,1,2,0:T(8,128)S(1)} fusion(f32[1,72,16,128]{3,1,2,0:T(8,128)S(1)} %convolution_bitcast_fusion.2, f32[1,72,16,128]{3,1,2,0:T(8,128)} %copy-done.4, f32[1,72,16,128]{3,1,2,0:T(8,128)} %copy-done.6, f32[3,72,16,1]{3,1,2,0:T(8,128)} %copy.58, f32[3,72,16,1]{3,1,2,0:T(8,128)S(1)} %copy.56, ...), kind=kOutput, calls=%fused_computation.6 | convolution fusion | flops 130351104 | bytes 2555138 | tf_op jit(solution)/shard_map/rjk,rjtl->rktl/dot_general | solution.py:43
  152.8 1.8 collective-permute-start.16
  154.8 14.0 %collective-permute-done.16 = f32[1,72,16,128]{3,1,2,0:T(8,128)S(1)} collective-permute-done((f32[1,72,16,128]{3,1,2,0:T(8,128)S(1)}, f32[1,72,16,128]{3,1,2,0:T(8,128)S(1)}, u32[]{:S(2)}, u32[]{:S(2)}) %collective-permute-start.16) | collective-permute-done | bytes 589856 | tf_op jit(solution)/shard_map/ppermute | solution.py:18
  168.8 12.4 %collective-permute-done.15 = f32[1,72,16,128]{3,1,2,0:T(8,128)S(1)} collective-permute-done((f32[1,72,16,128]{3,1,2,0:T(8,128)S(1)}, f32[1,72,16,128]{3,1,2,0:T(8,128)S(1)}, u32[]{:S(2)}, u32[]{:S(2)}) %collective-permute-start.15) | collective-permute-done | bytes 589856 | tf_op jit(solution)/shard_map/ppermute | solution.py:15
  181.3 0.8 copy-done.7
  182.2 1.8 fusion.90
  184.1 2.0 copy.60
  186.1 0.6 copy.62
  186.7 0.5 collective-permute-start.18
  187.3 0.6 copy.61
  188.1 1.8 copy.63
  189.9 2.7 %convolution_bitcast_fusion = f32[1,72,16,128]{3,1,2,0:T(8,128)S(1)} fusion(f32[1,72,16,128]{3,1,2,0:T(8,128)S(1)} %convolution_bitcast_fusion.1, f32[1,72,16,128]{3,1,2,0:T(8,128)} %copy-done.5, f32[1,72,16,128]{3,1,2,0:T(8,128)} %copy-done.7, f32[3,72,16,1]{3,1,2,0:T(8,128)} %copy.63, f32[3,72,16,1]{3,1,2,0:T(8,128)S(1)} %copy.61, ...), kind=kOutput, calls=%fused_computation.5 | convolution fusion | flops 130351104 | bytes 2555138 | tf_op jit(solution)/shard_map/rjk,rjtl->rktl/dot_general | solution.py:43
  192.6 2.9 %collective-permute-start.20 = (f32[1,72,16,128]{3,1,2,0:T(8,128)S(1)}, f32[1,72,16,128]{3,1,2,0:T(8,128)S(1)}, u32[]{:S(2)}, u32[]{:S(2)}) collective-permute-start(f32[1,72,16,128]{3,1,2,0:T(8,128)S(1)} %convolution_bitcast_fusion), channel_id=1, source_target_pairs={{1,0},{2,1},{3,2},{8,3},{9,8},{10,9},{11,10},{16,11},{17,16},{18,1... | collective-permute-start | bytes 1769480 | tf_op jit(solution)/shard_map/ppermute | solution.py:18
  195.5 13.7 %collective-permute-done.20 = f32[1,72,16,128]{3,1,2,0:T(8,128)S(1)} collective-permute-done((f32[1,72,16,128]{3,1,2,0:T(8,128)S(1)}, f32[1,72,16,128]{3,1,2,0:T(8,128)S(1)}, u32[]{:S(2)}, u32[]{:S(2)}) %collective-permute-start.20) | collective-permute-done | bytes 589856 | tf_op jit(solution)/shard_map/ppermute | solution.py:18
  209.2 14.2 %collective-permute-done.19 = f32[1,72,16,128]{3,1,2,0:T(8,128)S(1)} collective-permute-done((f32[1,72,16,128]{3,1,2,0:T(8,128)S(1)}, f32[1,72,16,128]{3,1,2,0:T(8,128)S(1)}, u32[]{:S(2)}, u32[]{:S(2)}) %collective-permute-start.19) | collective-permute-done | bytes 589856 | tf_op jit(solution)/shard_map/ppermute | solution.py:15
  223.5 0.8 copy-done.3
  224.4 1.8 fusion.89
  226.3 2.0 copy.65
  228.3 0.6 copy.67
  228.9 0.5 collective-permute-start.22
  229.5 0.6 copy.66
  230.3 1.8 copy.68
  232.1 1.8 fusion.23
  234.1 19.1 %all_to_all.24 = f32[1,72,16,128]{3,2,0,1:T(8,128)S(1)} all-to-all(f32[1,72,16,128]{3,2,0,1:T(8,128)S(1)} %copy.69), channel_id=1, replica_groups=mesh['lat'=4,'lon'=2,'lev'=4] {'lev'}, dimensions={1} | all-to-all | bytes 1179648 | tf_op jit(solution)/shard_map/all_to_all | solution.py:101
  253.2 0.8 copy.133
  (60 shorter events, 4.9 us)
Async XLA Ops:
  0.0 66.7 %copy-start = (f32[1,72,72]{2,1,0:T(8,128)S(1)}, f32[1,72,72]{2,1,0:T(8,128)}, u32[]{:S(2)}) copy-start(f32[1,72,72]{2,1,0:T(8,128)} %param.8) | copy-start | bytes 62212
  1.4 44.9 %collective-permute-start.1 = (f32[64,16]{0,1:T(8,128)S(1)}, f32[64,16]{0,1:T(8,128)S(1)}, u32[]{:S(2)}, u32[]{:S(2)}) collective-permute-start(f32[64,16]{0,1:T(8,128)S(1)} %broadcast_multiply_fusion.2), channel_id=1, source_target_pairs={{0,7},{1,0},{2,1},{3,2},{4,3},{5,4},{6,5},{7,6},{8,15},{9,8},{10,9... | collective-permute-start | bytes 12296 | tf_op jit(solution)/shard_map/ppermute | solution.py:82
  5.9 12.9 %collective-permute-start = (f32[64,16]{0,1:T(8,128)S(1)}, f32[64,16]{0,1:T(8,128)S(1)}, u32[]{:S(2)}, u32[]{:S(2)}) collective-permute-start(f32[64,16]{0,1:T(8,128)S(1)} %broadcast_multiply_fusion.2), channel_id=1, source_target_pairs={{0,1},{1,2},{2,3},{3,4},{4,5},{5,6},{6,7},{7,0},{8,9},{9,10},{10,1... | collective-permute-start | bytes 12296 | tf_op jit(solution)/shard_map/ppermute | solution.py:79
  18.7 29.1 %collective-permute-start.2 = (f32[64,16]{0,1:T(8,128)S(1)}, f32[64,16]{0,1:T(8,128)S(1)}, u32[]{:S(2)}, u32[]{:S(2)}) collective-permute-start(f32[64,16]{0,1:T(8,128)S(1)} %collective-permute-done), channel_id=1, source_target_pairs={{0,1},{1,2},{2,3},{3,4},{4,5},{5,6},{6,7},{7,0},{8,9},{9,10},{10,1... | collective-permute-start | bytes 12296 | tf_op jit(solution)/shard_map/ppermute | solution.py:79
  46.3 3.7 %collective-permute-start.3 = (f32[64,16]{0,1:T(8,128)S(1)}, f32[64,16]{0,1:T(8,128)S(1)}, u32[]{:S(2)}, u32[]{:S(2)}) collective-permute-start(f32[64,16]{0,1:T(8,128)S(1)} %collective-permute-done.1), channel_id=1, source_target_pairs={{0,7},{1,0},{2,1},{3,2},{4,3},{5,4},{6,5},{7,6},{8,15},{9,8},{10,9... | collective-permute-start | bytes 12296 | tf_op jit(solution)/shard_map/ppermute | solution.py:82
  47.8 4.9 %collective-permute-start.4 = (f32[64,16]{0,1:T(8,128)S(1)}, f32[64,16]{0,1:T(8,128)S(1)}, u32[]{:S(2)}, u32[]{:S(2)}) collective-permute-start(f32[64,16]{0,1:T(8,128)S(1)} %collective-permute-done.2), channel_id=1, source_target_pairs={{0,1},{1,2},{2,3},{3,4},{4,5},{5,6},{6,7},{7,0},{8,9},{9,10},{10,1... | collective-permute-start | bytes 12296 | tf_op jit(solution)/shard_map/ppermute | solution.py:79
  49.9 4.6 %collective-permute-start.5 = (f32[64,16]{0,1:T(8,128)S(1)}, f32[64,16]{0,1:T(8,128)S(1)}, u32[]{:S(2)}, u32[]{:S(2)}) collective-permute-start(f32[64,16]{0,1:T(8,128)S(1)} %collective-permute-done.3), channel_id=1, source_target_pairs={{0,7},{1,0},{2,1},{3,2},{4,3},{5,4},{6,5},{7,6},{8,15},{9,8},{10,9... | collective-permute-start | bytes 12296 | tf_op jit(solution)/shard_map/ppermute | solution.py:82
  52.7 4.9 %collective-permute-start.6 = (f32[64,16]{0,1:T(8,128)S(1)}, f32[64,16]{0,1:T(8,128)S(1)}, u32[]{:S(2)}, u32[]{:S(2)}) collective-permute-start(f32[64,16]{0,1:T(8,128)S(1)} %collective-permute-done.4), channel_id=1, source_target_pairs={{0,1},{1,2},{2,3},{3,4},{4,5},{5,6},{6,7},{7,0},{8,9},{9,10},{10,1... | collective-permute-start | bytes 12296 | tf_op jit(solution)/shard_map/ppermute | solution.py:79
  67.5 30.1 %collective-permute-start.8 = (f32[1,72,16,128]{3,1,2,0:T(8,128)S(1)}, f32[1,72,16,128]{3,1,2,0:T(8,128)S(1)}, u32[]{:S(2)}, u32[]{:S(2)}) collective-permute-start(f32[1,72,16,128]{3,1,2,0:T(8,128)S(1)} %convolution_bitcast_fusion.3), channel_id=1, source_target_pairs={{1,0},{2,1},{3,2},{8,3},{9,8},{10,9},{11,10},{16,11},{17,16},{18,1... | collective-permute-start | bytes 1769480 | tf_op jit(solution)/shard_map/ppermute | solution.py:18
  70.8 26.9 %collective-permute-start.7 = (f32[1,72,16,128]{3,1,2,0:T(8,128)S(1)}, f32[1,72,16,128]{3,1,2,0:T(8,128)S(1)}, u32[]{:S(2)}, u32[]{:S(2)}) collective-permute-start(f32[1,72,16,128]{3,1,2,0:T(8,128)S(1)} %convolution_bitcast_fusion.3), channel_id=1, source_target_pairs={{0,1},{1,2},{2,3},{3,8},{8,9},{9,10},{10,11},{11,16},{16,17},{17,1... | collective-permute-start | bytes 1769480 | tf_op jit(solution)/shard_map/ppermute | solution.py:15
  70.8 26.8 %all-to-all-start = ((f32[4,18,2,128]{3,2,1,0:T(2,128)}), f32[4,18,2,128]{3,2,1,0:T(2,128)S(1)}, u32[]{:S(2)}, u32[]{:S(2)}) async-start(f32[4,18,2,128]{3,2,1,0:T(2,128)} %param.7), calls=%async_computation | async-start | bytes 147456 | tf_op jit(solution)/shard_map/all_to_all | solution.py:92
  97.6 0.8 copy-start.1
  98.4 0.8 copy-start.2
  103.8 2.0 collective-permute-start.10
  103.9 1.3 collective-permute-start.9
  110.3 17.8 %collective-permute-start.12 = (f32[1,72,16,128]{3,1,2,0:T(8,128)S(1)}, f32[1,72,16,128]{3,1,2,0:T(8,128)S(1)}, u32[]{:S(2)}, u32[]{:S(2)}) collective-permute-start(f32[1,72,16,128]{3,1,2,0:T(8,128)S(1)} %convolution_bitcast_fusion.2), channel_id=1, source_target_pairs={{1,0},{2,1},{3,2},{8,3},{9,8},{10,9},{11,10},{16,11},{17,16},{18,1... | collective-permute-start | bytes 1769480 | tf_op jit(solution)/shard_map/ppermute | solution.py:18
  114.5 26.9 %collective-permute-start.11 = (f32[1,72,16,128]{3,1,2,0:T(8,128)S(1)}, f32[1,72,16,128]{3,1,2,0:T(8,128)S(1)}, u32[]{:S(2)}, u32[]{:S(2)}) collective-permute-start(f32[1,72,16,128]{3,1,2,0:T(8,128)S(1)} %convolution_bitcast_fusion.2), channel_id=1, source_target_pairs={{0,1},{1,2},{2,3},{3,8},{8,9},{9,10},{10,11},{11,16},{16,17},{17,1... | collective-permute-start | bytes 1769480 | tf_op jit(solution)/shard_map/ppermute | solution.py:15
  128.2 13.2 %copy-start.4 = (f32[1,72,16,128]{3,1,2,0:T(8,128)}, f32[1,72,16,128]{3,1,2,0:T(8,128)S(1)}, u32[]{:S(2)}) copy-start(f32[1,72,16,128]{3,1,2,0:T(8,128)S(1)} %collective-permute-done.12) | copy-start | bytes 1769476
  141.4 0.8 copy-start.6
  146.2 1.2 collective-permute-start.13
  146.9 1.4 collective-permute-start.14
  152.8 16.1 %collective-permute-start.16 = (f32[1,72,16,128]{3,1,2,0:T(8,128)S(1)}, f32[1,72,16,128]{3,1,2,0:T(8,128)S(1)}, u32[]{:S(2)}, u32[]{:S(2)}) collective-permute-start(f32[1,72,16,128]{3,1,2,0:T(8,128)S(1)} %convolution_bitcast_fusion.1), channel_id=1, source_target_pairs={{1,0},{2,1},{3,2},{8,3},{9,8},{10,9},{11,10},{16,11},{17,16},{18,1... | collective-permute-start | bytes 1769480 | tf_op jit(solution)/shard_map/ppermute | solution.py:18
  154.6 26.7 %collective-permute-start.15 = (f32[1,72,16,128]{3,1,2,0:T(8,128)S(1)}, f32[1,72,16,128]{3,1,2,0:T(8,128)S(1)}, u32[]{:S(2)}, u32[]{:S(2)}) collective-permute-start(f32[1,72,16,128]{3,1,2,0:T(8,128)S(1)} %convolution_bitcast_fusion.1), channel_id=1, source_target_pairs={{0,1},{1,2},{2,3},{3,8},{8,9},{9,10},{10,11},{11,16},{16,17},{17,1... | collective-permute-start | bytes 1769480 | tf_op jit(solution)/shard_map/ppermute | solution.py:15
  168.8 12.4 %copy-start.5 = (f32[1,72,16,128]{3,1,2,0:T(8,128)}, f32[1,72,16,128]{3,1,2,0:T(8,128)S(1)}, u32[]{:S(2)}) copy-start(f32[1,72,16,128]{3,1,2,0:T(8,128)S(1)} %collective-permute-done.16) | copy-start | bytes 1769476
  181.3 0.8 copy-start.7
  186.1 1.2 collective-permute-start.17
  186.7 1.4 collective-permute-start.18
  192.6 16.6 %collective-permute-start.20 = (f32[1,72,16,128]{3,1,2,0:T(8,128)S(1)}, f32[1,72,16,128]{3,1,2,0:T(8,128)S(1)}, u32[]{:S(2)}, u32[]{:S(2)}) collective-permute-start(f32[1,72,16,128]{3,1,2,0:T(8,128)S(1)} %convolution_bitcast_fusion), channel_id=1, source_target_pairs={{1,0},{2,1},{3,2},{8,3},{9,8},{10,9},{11,10},{16,11},{17,16},{18,1... | collective-permute-start | bytes 1769480 | tf_op jit(solution)/shard_map/ppermute | solution.py:18
  195.5 27.9 %collective-permute-start.19 = (f32[1,72,16,128]{3,1,2,0:T(8,128)S(1)}, f32[1,72,16,128]{3,1,2,0:T(8,128)S(1)}, u32[]{:S(2)}, u32[]{:S(2)}) collective-permute-start(f32[1,72,16,128]{3,1,2,0:T(8,128)S(1)} %convolution_bitcast_fusion), channel_id=1, source_target_pairs={{0,1},{1,2},{2,3},{3,8},{8,9},{9,10},{10,11},{11,16},{16,17},{17,1... | collective-permute-start | bytes 1769480 | tf_op jit(solution)/shard_map/ppermute | solution.py:15
  223.4 0.8 copy-start.3
  228.3 1.2 collective-permute-start.21
  228.9 1.4 collective-permute-start.22
